TPU v7x, 32 devices: a whole 2x2x4 slice. The times are simulated.
32 devices in a mesh: group: 2 (over y), seq: 4 (over z), blk: 2 (over x), tp: 2 (over core).
Axes of the slice: x: 2, y: 2, z: 4, core: 2. Of those that a mesh axis runs over, the one named last changes fastest.
Arguments:
- tokens: bfloat16 [2048, 3072], P(('group', 'blk'), ('seq', 'tp')), parts along dimension 0, may hold values from -64 to 64
- timestep: int32 [2], P('group'), parts along dimension 0, may hold values from 25 to 49
- padded_heads: int32 [2], P('group'), parts along dimension 0, may hold values from 1 to 3
- modulation: float32 [50, 3, 3072], replicated, may hold values from -3 to 3
- qkv_weight: bfloat16 [3, 3072, 1024], P(None, 'blk', ('seq', 'tp')), may hold values from -1 to 1
- out_weight: bfloat16 [1024, 3072], P(('seq', 'tp'), 'blk'), may hold values from -0.5 to 0.5
Outputs:
- update: bfloat16 [2048, 3072], P(('group', 'blk'), ('seq', 'tp')), parts along dimension 0
There are 2 independent parts, one for each index of `group`. A program takes and returns all parts, laid end to end along the dimension named above; an argument that names none is the same for every part. Nothing has to cross between parts.
All inputs are finite; a program needn't handle non-finite values.
Results may differ from a plain program's by a relative error of at most 0.023.
Values may be sent and summed in bfloat16 or wider, within the bound.
A program may use at most 64 MiB of HBM per device.

v0:
```python
import math

import jax
import jax.numpy as jnp
from jax import lax
from jax.sharding import PartitionSpec as P

epsilon = 1e-06
neg_large = -1e30


def collect(own_part):
    gathered = lax.all_gather(own_part, ("seq", "tp"), axis=1, tiled=True)
    return gathered


def attend_block(running, queries, key_block, value_block, factor):
    largest, totals, weighted = running
    scores = (
        lax.dot_general(
            queries, key_block, (((1,), (1,)), ((), ())), preferred_element_type=jnp.float32
        )
        * factor
    )
    new_max = jnp.maximum(largest, jnp.max(scores, axis=1))
    rescale = jnp.exp(largest - new_max)
    weights = jnp.exp(scores - new_max[:, None])
    totals = totals * rescale + jnp.sum(weights, axis=1)
    weighted = weighted * rescale[:, None] + jnp.dot(
        weights.astype(jnp.bfloat16), value_block, preferred_element_type=jnp.float32
    )
    return (new_max, totals, weighted)


def body(tokens, timestep, padded_heads, modulation, qkv_weight, out_weight):
    slices = lax.axis_size(("seq", "tp"))
    own_index = lax.axis_index(("seq", "tp"))
    model_width = modulation.shape[2]
    own_width = model_width // slices
    token_rows = tokens.shape[0]
    head_size = out_weight.shape[0]
    table_row = lax.dynamic_index_in_dim(modulation, timestep[0], 0, keepdims=False)
    own_entry = lax.dynamic_slice_in_dim(table_row, own_index * own_width, own_width, 1)
    gathered = collect(tokens).astype(jnp.float32)
    average = jnp.mean(gathered, axis=1, keepdims=True)
    centered = gathered - average
    spread = jnp.mean(centered * centered, axis=1, keepdims=True)
    normed = centered * lax.rsqrt(spread + epsilon)
    modulated = (normed * (1.0 + table_row[1]) + table_row[0]).astype(jnp.bfloat16)
    projected = jnp.einsum(
        "td,kde->kte",
        modulated,
        lax.all_gather(qkv_weight, "blk", axis=1, tiled=True),
        preferred_element_type=jnp.float32,
    ).astype(jnp.bfloat16)
    queries = projected[0]
    factor = 1.0 / math.sqrt(head_size)
    initial = (
        jnp.full((token_rows,), neg_large, jnp.float32),
        jnp.zeros((token_rows,), jnp.float32),
        jnp.zeros((token_rows, head_size), jnp.float32),
    )
    key_piece = lax.all_gather(projected[1], "blk", axis=0, tiled=True)
    value_piece = lax.all_gather(projected[2], "blk", axis=0, tiled=True)
    length = key_piece.shape[0]

    def one_block(counter, inner_state):
        key_block = lax.dynamic_slice_in_dim(key_piece, counter * 512, 512, 0)
        value_block = lax.dynamic_slice_in_dim(value_piece, counter * 512, 512, 0)
        return attend_block(inner_state, queries, key_block, value_block, factor)

    largest, exp_totals, weighted = lax.fori_loop(0, length // 512, one_block, initial)
    attended = weighted / exp_totals[:, None]
    live_heads = slices - padded_heads[0]
    masked = jnp.where(own_index < live_heads, attended, 0.0).astype(jnp.bfloat16)
    head_term = jnp.dot(
        masked,
        lax.all_gather(out_weight, "blk", axis=1, tiled=True),
        preferred_element_type=jnp.float32,
    )
    summed = lax.psum_scatter(
        head_term.astype(jnp.bfloat16), ("seq", "tp"), scatter_dimension=1, tiled=True
    ).astype(jnp.float32)
    return (own_entry[2] * summed).astype(jnp.bfloat16)


def solution(mesh):
    return jax.shard_map(
        body,
        mesh=mesh,
        in_specs=(
            P(("group", "blk"), ("seq", "tp")),
            P("group"),
            P("group"),
            P(),
            P(None, "blk", ("seq", "tp")),
            P(("seq", "tp"), "blk"),
        ),
        out_specs=P(("group", "blk"), ("seq", "tp")),
        check_vma=False,
    )
```

profile of v0, /device:TPU:0, one launch (start us, length us, event | category | flops | bytes accessed | tf_op | source)
XLA Modules:
  0.0 157.3 jit_solution(16973399973763437814)
XLA Ops:
  6.5 0.0 all-gather.5.cloned.1.call-start
  6.5 0.7 all-gather.5.cloned.1.call-update
  7.3 0.0 all-gather.7.cloned.1.call-start
  7.3 0.7 all-gather.7.cloned.1.call-update
  8.0 0.0 reduce-scatter.4.cloned.1.call-start
  9.4 14.8 %all_gather.19 = bf16[128,3072]{1,0:T(8,128)(2,1)} all-gather(bf16[128,1536]{1,0:T(8,128)(2,1)} %param.13), channel_id=1, replica_groups=mesh['group'=2,'seq'=4,'blk'=2,'tp'=2] {'blk'}, dimensions={1}, use_global_device_ids=true | all-gather | bytes 1179648 | tf_op jit(solution)/shard_map/all_gather | solution.py:78
  24.1 1.0 dynamic-slice_add_fusion
  25.1 24.4 %all-gather.5.cloned.1.call-done = bf16[512,3072]{1,0:T(8,128)(2,1)} async-done(((bf16[512,384]{1,0:T(8,128)(2,1)}), bf16[512,3072]{1,0:T(8,128)(2,1)}) %all-gather.5.cloned.1.call-update) | async-done | bytes 3145744 | tf_op jit(solution)/shard_map/all_gather | solution.py:13
  49.5 0.0 copy-start
  49.5 2.5 %convert_reduce_fusion = f32[512]{0:T(512)S(1)} fusion(bf16[512,3072]{1,0:T(8,128)(2,1)} %all-gather.5.cloned.1.call-done), kind=kLoop, calls=%fused_computation.16 | loop fusion | flops 3145216 | bytes 3147776 | tf_op jit(solution)/shard_map/reduce_sum | solution.py:45
  52.0 0.3 copy-done
  52.3 1.0 fusion.11
  53.3 33.1 %all-gather.7.cloned.1.call-done = bf16[3,3072,128]{2,1,0:T(8,128)(2,1)} async-done(((bf16[3,1536,128]{2,1,0:T(8,128)(2,1)}), bf16[3,3072,128]{2,1,0:T(8,128)(2,1)}) %all-gather.7.cloned.1.call-update) | async-done | bytes 2359312 | tf_op jit(solution)/shard_map/all_gather | solution.py:53
  86.4 3.5 %fusion.21 = bf16[3,512,128]{2,1,0:T(8,128)(2,1)S(1)} fusion(bf16[3,3072,128]{2,1,0:T(8,128)(2,1)} %all-gather.7.cloned.1.call-done, bf16[512,3072]{1,0:T(8,128)(2,1)S(1)} %copy-done, f32[3072]{0:T(1024)S(1)} %bitcast.32, f32[3072]{0:T(1024)S(1)} %bitcast.31, f32[512]{0:T(512)S(1)} %add_rsqrt_fusion, f32[512]{0:T(512)S(1)} %broadcast_multiply_fusion), kind=kOutput, calls=%fused_computation.27 | convolution fusion | flops 1217593344 | bytes 5926912 | tf_op jit(solution)/shard_map/td,kde->kte/dot_general | solution.py:50
  90.0 5.7 %all-gather = bf16[1,1024,128]{2,1,0:T(8,128)(2,1)S(1)} all-gather(bf16[1,512,128]{2,1,0:T(8,128)(2,1)S(1)} %get-tuple-element.178), channel_id=2, replica_groups=mesh['group'=2,'seq'=4,'blk'=2,'tp'=2] {'blk'}, dimensions={1}, use_global_device_ids=true | all-gather | bytes 393216 | tf_op jit(solution)/shard_map/all_gather | solution.py:63
  95.7 5.6 %all-gather.1 = bf16[1,1024,128]{2,1,0:T(8,128)(2,1)S(1)} all-gather(bf16[1,512,128]{2,1,0:T(8,128)(2,1)S(1)} %get-tuple-element.176), channel_id=3, replica_groups=mesh['group'=2,'seq'=4,'blk'=2,'tp'=2] {'blk'}, dimensions={1}, use_global_device_ids=true | all-gather | bytes 393216 | tf_op jit(solution)/shard_map/all_gather | solution.py:64
  101.3 1.9 %while.18 = (s32[]{:T(128)}, f32[512]{0:T(512)S(1)}, f32[512]{0:T(512)S(1)}, f32[512,128]{1,0:T(8,128)S(1)}, bf16[1024,128]{1,0:T(8,128)(2,1)S(1)}, /*index=5*/b...) while((s32[]{:T(128)}, f32[512]{0:T(512)S(1)}, ...), condition=%wide.region_5.6_spmd.clone, body=%wide.region_2.5_spmd.clone.sunk | while | flops 135989760 | bytes 4096175 | solution.py:72
  101.3 0.3 fusion.42
  101.7 0.2 fusion.43
  101.9 0.4 convolution_add_fusion.2
  102.3 0.3 fusion.42
  102.6 0.2 fusion.43
  102.8 0.4 convolution_add_fusion.2
  103.2 2.2 %convolution_convert_fusion = bf16[512,3072]{1,0:T(8,128)(2,1)S(1)} fusion(bf16[128,3072]{1,0:T(8,128)(2,1)} %all_gather.19, f32[512,128]{1,0:T(8,128)S(1)} %get-tuple-element.130, f32[512]{0:T(512)S(1)} %get-tuple-element.131, pred[]{:T(512)S(6)} %lt.25), kind=kOutput, calls=%fused_computation.23 | convolution fusion | flops 404422656 | bytes 4196353 | tf_op jit(solution)/shard_map/dot_general | solution.py:76
  105.4 2.8 %copy.7 = bf16[512,3072]{0,1:T(8,128)(2,1)} copy(bf16[512,3072]{1,0:T(8,128)(2,1)S(1)} %convolution_convert_fusion) | data formatting | bytes 6291456
  108.2 0.0 reduce-scatter.4.cloned.1.call-update
  108.3 0.8 dynamic-slice_reduce_fusion
  109.1 39.7 %reduce-scatter.4.cloned.1.call-done = bf16[384,512]{1,0:T(8,128)(2,1)} async-done(((bf16[3072,512]{1,0:T(8,128)(2,1)}), bf16[384,512]{1,0:T(8,128)(2,1)}) %reduce-scatter.4.cloned.1.call-update) | async-done | bytes 393232
  148.8 1.2 copy.8
  150.0 0.8 multiply_convert_fusion
  (12 shorter events, 0.1 us)
Async XLA Ops:
  6.5 42.9 %all-gather.5.cloned.1.call-start = ((), (), s32[]{:S(2)}) async-start(), calls=%async_computation.1 | async-start | bytes 3538944 | tf_op jit(solution)/shard_map/all_gather | solution.py:13
  7.3 79.2 %all-gather.7.cloned.1.call-start = ((), (), s32[]{:S(2)}) async-start(), calls=%async_computation.2 | async-start | bytes 3538944 | tf_op jit(solution)/shard_map/all_gather | solution.py:53
  8.0 140.8 %reduce-scatter.4.cloned.1.call-start = ((), (), s32[]{:S(2)}) async-start(), calls=%async_computation.3 | async-start | bytes 3538944
  49.5 2.8 %copy-start = (bf16[512,3072]{1,0:T(8,128)(2,1)S(1)}, bf16[512,3072]{1,0:T(8,128)(2,1)}, u32[]{:S(2)}) copy-start(bf16[512,3072]{1,0:T(8,128)(2,1)} %all-gather.5.cloned.1.call-done) | copy-start | bytes 9437188
Sparse Core Ops, SparseCore 0:
  8.9 40.4 all-gather.4
  51.0 35.3 all-gather.6
  108.4 40.3 reduce-scatter.3
where the time goes:
time: 158 us; the launch traced here: 157 us
  waiting for transfers between devices  98.6 us (62%)
  blocking collectives  26.1 us (17%)
  between operations  14.5 us (9%)
  matrix products  7.03 us (4%)
  other arithmetic  5.73 us (4%)
  local copies, waits for them, and re-layouts  5.18 us (3%)
    unnamed x4, waiting for transfers between devices  41.1 us
    all_gather x1, waiting for transfers between devices, body(): lax.all_gather(qkv_weight, 'blk', axis=1, tiled=True)  33.1 us
    all_gather x1, waiting for transfers between devices, collect(): gathered = lax.all_gather(own_part, ('seq', 'tp'), axis=1, tiled=True)  24.4 us
    all_gather x1, blocking collectives, body(): lax.all_gather(out_weight, 'blk', axis=1, tiled=True)  14.8 us
    all_gather x1, blocking collectives, body(): key_piece = lax.all_gather(projected[1], 'blk', axis=0, tiled=True)  5.73 us
    all_gather x1, blocking collectives, body(): value_piece = lax.all_gather(projected[2], 'blk', axis=0, tiled=True)  5.62 us
    unnamed x4, local copies, waits for them, and re-layouts  4.33 us
    dot_general x1, matrix products, body(): jnp.einsum('td,kde->kte', modulated, lax.all_gather(qkv_weight, 'blk', ax...  3.52 us
  transfers between devices with their start and end apart: 3, of which 3 were waited for; matrix products, arithmetic and copies ran while one was open for 3% of the time, Pallas kernels for 0%

commit v1 on v0

--- a/solution.py
+++ b/solution.py
@@ -1,8 +1,11 @@
+import functools
 import math
 
 import jax
 import jax.numpy as jnp
 from jax import lax
+from jax.experimental import pallas as pl
+from jax.experimental.pallas import tpu as pltpu
 from jax.sharding import PartitionSpec as P
 
 epsilon = 1e-06
@@ -84,9 +87,396 @@
     return (own_entry[2] * summed).astype(jnp.bfloat16)
 
 
+MESH = pl.DeviceIdType.MESH
+bf16, f32 = jnp.bfloat16, jnp.float32
+
+
+def fused_kernel(
+    dims,
+    tokens_ref,
+    table_ref,
+    qkv_ref,
+    out_weight_ref,
+    out_ref,
+    tok,
+    mod,
+    wts,
+    query,
+    kv,
+    att,
+    wout,
+    local_sem,
+    tok_send,
+    tok_recv,
+    w_send,
+    w_recv,
+    kv_send,
+    kv_recv,
+    att_send,
+    att_recv,
+    o_send,
+    o_recv,
+    f_send,
+    f_recv,
+):
+    S, chunks, pieces = dims
+    rows, width = tokens_ref.shape
+    kinds, half, size = qkv_ref.shape
+    slices = 2 * S
+    g, z = lax.axis_index("group"), lax.axis_index("seq")
+    x, c = lax.axis_index("blk"), lax.axis_index("tp")
+    own = z * 2 + c
+    R = rows // chunks
+    A = rows // pieces
+    part = half // 2
+    hpart = size // 2
+
+    up, down = (g, z + 1, x, c), (g, z - 1, x, c)
+    mate = (g, z, x, 1 - c)
+    over = (g, z, 1 - x, c)
+    twin = (1 - g, z, x, c)
+
+    def remote(src, dst, s_sem, r_sem, where):
+        return pltpu.make_async_remote_copy(
+            src_ref=src,
+            dst_ref=dst,
+            send_sem=s_sem,
+            recv_sem=r_sem,
+            device_id=where,
+            device_id_type=MESH,
+        )
+
+    def lanes(index, extent):
+        return pl.ds(pl.multiple_of(index * extent, 128), extent)
+
+    def tok_at(s, r):
+        return tok.at[pl.ds(r * R, R), lanes(s, width)]
+
+    def att_at(s, r):
+        return att.at[pl.ds(r * A, A), lanes(s, size)]
+
+    def tok_copy(way, s, r, where, src=None):
+        there = tok_at(s, r)
+        return remote(there if src is None else src, there, tok_send.at[way, s, r], tok_recv.at[s, r], where)
+
+    def att_copy(way, s, r, where, src=None):
+        there = att_at(s, r)
+        return remote(there, there, att_send.at[way, s, r], att_recv.at[s, r], where)
+
+    def send_own(make, r, src=None):
+        @pl.when(z < S - 1)
+        def _():
+            make(0, own, r, up, src).start()
+
+        @pl.when(z > 0)
+        def _():
+            make(1, own, r, down, src).start()
+
+        make(2, own, r, mate, src).start()
+
+    def relay(make, d, r):
+        @pl.when(z - d >= 0)
+        def _():
+            s = (z - d) * 2 + c
+            make(0, s, r, up).wait_recv()
+
+            @pl.when(z < S - 1)
+            def _():
+                make(0, s, r, up).start()
+
+            make(2, s, r, mate).start()
+
+        @pl.when(z + d < S)
+        def _():
+            s = (z + d) * 2 + c
+            make(1, s, r, down).wait_recv()
+
+            @pl.when(z > 0)
+            def _():
+                make(1, s, r, down).start()
+
+            make(2, s, r, mate).start()
+
+    def wait_mates(make, r):
+        for other in range(S):
+            make(2, other * 2 + 1 - c, r, mate).wait_recv()
+
+    def drain(make, count):
+        for r in range(count):
+            for other in range(S):
+                s = other * 2 + c
+
+                @pl.when((z < S - 1) & (other <= z))
+                def _():
+                    make(0, s, r, up).wait_send()
+
+                @pl.when((z > 0) & (other >= z))
+                def _():
+                    make(1, s, r, down).wait_send()
+
+                make(2, s, r, mate).wait_send()
+
+    def w_at(block, p, i):
+        first = pl.multiple_of(block * half + p * part, 16)
+        return wts.at[pl.ds(first, part), pl.ds(i * size, size)]
+
+    def w_over(i):
+        src = qkv_ref.at[i, pl.ds(pl.multiple_of(g * part, 16), part)]
+        return remote(src, w_at(x, g, i), w_send.at[0, i], w_recv.at[0, i], over)
+
+    def w_over_in(i):
+        there = w_at(1 - x, g, i)
+        return remote(there, there, w_send.at[0, i], w_recv.at[0, i], over)
+
+    def w_twin(i):
+        there = w_at(1 - x, g, i)
+        return remote(there, there, w_send.at[1, i], w_recv.at[1, i], twin)
+
+    def w_twin_in(i):
+        there = w_at(1 - x, 1 - g, i)
+        return remote(there, there, w_send.at[1, i], w_recv.at[1, i], twin)
+
+    def o_at(head, p):
+        return wout.at[head, pl.ds(pl.multiple_of(p * hpart, 16), hpart)]
+
+    def o_src(j):
+        return out_weight_ref.at[pl.ds(pl.multiple_of(g * hpart, 16), hpart), pl.ds(j * width, width)]
+
+    per_blk = slices // 2
+    home = own // per_blk == x
+
+    def o_copy(j):
+        s = x * per_blk + j
+        return remote(o_src(j), o_at(own, g), o_send.at[j], o_recv.at[own], (g, s // 2, x, s % 2))
+
+    def o_local(j):
+        return pltpu.make_async_copy(o_src(j), o_at(own, g), local_sem.at[5])
+
+    def o_in(head):
+        return remote(o_at(head, g), o_at(head, g), o_send.at[0], o_recv.at[head], mate)
+
+    def o_all(p):
+        return wout.at[:, pl.ds(pl.multiple_of(p * hpart, 16), hpart)]
+
+    def f_over():
+        return remote(o_all(g), o_all(g), f_send.at[0], f_recv.at[0], over)
+
+    def f_twin():
+        return remote(o_all(g), o_all(g), f_send.at[1], f_recv.at[1], twin)
+
+    def f_twin_in():
+        return remote(o_all(1 - g), o_all(1 - g), f_send.at[1], f_recv.at[1], twin)
+
+    def kv_at(block, r):
+        return kv.at[block, :, pl.ds(r * R, R)]
+
+    def kv_copy(block, r):
+        return remote(kv_at(block, r), kv_at(block, r), kv_send.at[r], kv_recv.at[r], over)
+
+    barrier = pltpu.get_barrier_semaphore()
+    for step in range(1, slices):
+        s = lax.rem(own + step, slices)
+        pl.semaphore_signal(barrier, inc=1, device_id=(g, s // 2, x, s % 2), device_id_type=MESH)
+    for where in (over, twin):
+        pl.semaphore_signal(barrier, inc=1, device_id=where, device_id_type=MESH)
+    locals_ = [pltpu.make_async_copy(tokens_ref, tok.at[:, lanes(own, width)], local_sem.at[0])]
+    for i in range(kinds):
+        there = wts.at[pl.ds(pl.multiple_of(x * half, 16), half), pl.ds(i * size, size)]
+        locals_.append(pltpu.make_async_copy(qkv_ref.at[i], there, local_sem.at[1 + i]))
+    for copy in locals_:
+        copy.start()
+    pl.semaphore_wait(barrier, slices + 1)
+
+    for r in range(chunks):
+        send_own(tok_copy, r, tokens_ref.at[pl.ds(r * R, R)])
+    for i in range(kinds):
+        w_over(i).start()
+    for copy in locals_:
+        copy.wait()
+
+    def normalise(r):
+        group_rows = 16
+
+        def one(i, carry):
+            at = pl.multiple_of(r * R + i * group_rows, group_rows)
+            values = tok[pl.ds(at, group_rows), :].astype(f32)
+            centered = values - jnp.mean(values, axis=1, keepdims=True)
+            spread = jnp.mean(centered * centered, axis=1, keepdims=True)
+            normed = centered * lax.rsqrt(spread + epsilon)
+            to = pl.multiple_of(i * group_rows, group_rows)
+            mod[pl.ds(to, group_rows), :] = (normed * (1.0 + table_ref[1:2, :]) + table_ref[0:1, :]).astype(bf16)
+            return carry
+
+        lax.fori_loop(0, R // group_rows, one, 0)
+
+    def compute(r):
+        wait_mates(tok_copy, r)
+        normalise(r)
+        if r == 0:
+            for i in range(kinds):
+                w_twin_in(i).wait_recv()
+        projected = jnp.dot(mod[...], wts[...], preferred_element_type=f32).astype(bf16)
+        query[pl.ds(r * R, R), :] = projected[:, :size]
+        kv[x, 0, pl.ds(r * R, R), :] = projected[:, size : 2 * size]
+        kv[x, 1, pl.ds(r * R, R), :] = projected[:, 2 * size :]
+        kv_copy(x, r).start()
+
+    forwarded = 0
+    for d in range(1, S):
+        last = d == S - 1
+        for r in range(chunks):
+            relay(tok_copy, d, r)
+            if r % 2 == 1 and forwarded < kinds:
+                w_over_in(forwarded).wait_recv()
+                w_twin(forwarded).start()
+                forwarded += 1
+            if last and r > 0:
+                compute(r - 1)
+        if d == S - 2:
+            for j in range(per_blk):
+                s = x * per_blk + j
+
+                @pl.when(s == own)
+                def _():
+                    o_local(j).start()
+
+                @pl.when(s != own)
+                def _():
+                    o_copy(j).start()
+
+    compute(chunks - 1)
+    for j in range(per_blk):
+        s = x * per_blk + j
+
+        @pl.when(s == own)
+        def _():
+            o_local(j).wait()
+
+    for r in range(chunks):
+        kv_copy(1 - x, r).wait_recv()
+
+    factor = 1.0 / math.sqrt(size)
+    contract = (((1,), (1,)), ((), ()))
+
+    def attend(r):
+        q = query[pl.ds(r * A, A), :]
+        scores = [
+            lax.dot_general(q, kv[b, 0], contract, preferred_element_type=f32) * factor for b in range(2)
+        ]
+        largest = jnp.maximum(
+            jnp.max(scores[0], axis=1, keepdims=True), jnp.max(scores[1], axis=1, keepdims=True)
+        )
+        total, weighted = 0.0, 0.0
+        for b in range(2):
+            weights = jnp.exp(scores[b] - largest)
+            total = total + jnp.sum(weights, axis=1, keepdims=True)
+            weighted = weighted + jnp.dot(weights.astype(bf16), kv[b, 1], preferred_element_type=f32)
+        attended = weighted / total
+        masked = jnp.where(table_ref[3:4, :size] > 0.0, attended, 0.0).astype(bf16)
+        att[pl.ds(r * A, A), lanes(own, size)] = masked
+        send_own(att_copy, r)
+
+    for r in range(pieces):
+        attend(r)
+
+    @pl.when(home)
+    def _():
+        for step in range(1, slices):
+            o_in(lax.rem(own + step, slices)).wait_recv()
+        f_over().start()
+        f_twin().start()
+
+    for d in range(1, S):
+        for r in range(pieces):
+            relay(att_copy, d, r)
+        if d == 1:
+
+            @pl.when(jnp.logical_not(home))
+            def _():
+                f_over().wait_recv()
+                f_twin().start()
+
+    f_twin_in().wait_recv()
+    gate = table_ref[2:3, lanes(own, width)]
+    weight = wout[...].reshape(slices * size, width)
+    for r in range(pieces):
+        wait_mates(att_copy, r)
+        summed = jnp.dot(att[pl.ds(r * A, A), :], weight, preferred_element_type=f32)
+        out_ref[pl.ds(r * A, A), :] = (gate * summed).astype(bf16)
+
+    drain(tok_copy, chunks)
+    drain(att_copy, pieces)
+    for i in range(kinds):
+        w_over(i).wait_send()
+        w_twin(i).wait_send()
+    for r in range(chunks):
+        kv_copy(x, r).wait_send()
+    for j in range(per_blk):
+        s = x * per_blk + j
+
+        @pl.when(s != own)
+        def _():
+            o_copy(j).wait_send()
+
+    f_twin().wait_send()
+
+    @pl.when(home)
+    def _():
+        f_over().wait_send()
+
+
+def fused_body(S, tokens, timestep, padded_heads, modulation, qkv_weight, out_weight):
+    slices = 2 * S
+    rows, width = tokens.shape
+    kinds, half, size = qkv_weight.shape
+    model_width = modulation.shape[2]
+    chunks, pieces = 4, 2
+    table_row = lax.dynamic_index_in_dim(modulation, timestep[0], 0, keepdims=False)
+    live = lax.axis_index(("seq", "tp")) < slices - padded_heads[0]
+    table = jnp.concatenate([table_row, jnp.full((1, model_width), live.astype(f32))], axis=0)
+    anywhere = pl.BlockSpec(memory_space=pl.ANY)
+    vmem = pl.BlockSpec(memory_space=pltpu.VMEM)
+    dma = pltpu.SemaphoreType.DMA
+    return pl.pallas_call(
+        functools.partial(fused_kernel, (S, chunks, pieces)),
+        out_shape=jax.ShapeDtypeStruct((rows, width), bf16),
+        in_specs=[anywhere, vmem, anywhere, anywhere],
+        out_specs=vmem,
+        scratch_shapes=[
+            pltpu.VMEM((rows, model_width), bf16),
+            pltpu.VMEM((rows // chunks, model_width), bf16),
+            pltpu.VMEM((model_width, kinds * size), bf16),
+            pltpu.VMEM((rows, size), bf16),
+            pltpu.VMEM((2, 2, rows, size), bf16),
+            pltpu.VMEM((rows, slices * size), bf16),
+            pltpu.VMEM((slices, size, width), bf16),
+            dma((6,)),
+            dma((3, slices, chunks)),
+            dma((slices, chunks)),
+            dma((2, kinds)),
+            dma((2, kinds)),
+            dma((chunks,)),
+            dma((chunks,)),
+            dma((3, slices, pieces)),
+            dma((slices, pieces)),
+            dma((slices // 2,)),
+            dma((slices,)),
+            dma((2,)),
+            dma((2,)),
+        ],
+        compiler_params=pltpu.CompilerParams(collective_id=0, has_side_effects=True),
+    )(tokens, table, qkv_weight, out_weight)
+
+
+def fits(mesh):
+    shape = mesh.shape
+    return shape["group"] == 2 and shape["blk"] == 2 and shape["tp"] == 2 and shape["seq"] >= 3
+
+
 def solution(mesh):
+    chosen = functools.partial(fused_body, mesh.shape["seq"]) if fits(mesh) else body
     return jax.shard_map(
-        body,
+        chosen,
         mesh=mesh,
         in_specs=(
             P(("group", "blk"), ("seq", "tp")),

time: 158 us -> 70.7 us (0.45)
  the two profiles are of different devices: /device:TPU:0 before, /device:TPU:2 now
where the time goes in v1:
time: 70.7 us; the launch traced here: 70.5 us
  Pallas kernels  66.4 us (94%)
  local copies, waits for them, and re-layouts  2.6 us (4%)
  between operations  1.47 us (2%)
    pallas_call x1, Pallas kernels, fused_body(): pl.pallas_call(functools.partial(fused_kernel, (S, chunks, pieces)), out_...  66.4 us
    unnamed x4, local copies, waits for them, and re-layouts  1.94 us

profile of v1, /device:TPU:2, one launch (start us, length us, event | category | flops | bytes accessed | tf_op | source)
XLA Modules:
  0.0 70.5 jit_solution(8797335076066231324)
XLA Ops:
  0.0 0.0 copy-start
  1.5 0.1 copy-done
  1.7 0.6 concatenate.3.table_ref
  2.3 66.4 %shard_map.64 = bf16[512,384]{1,0:T(8,128)(2,1)} custom-call(bf16[512,384]{1,0:T(8,128)(2,1)} %tokens_ref.1, f32[4,3072]{1,0:T(4,128)} %concatenate.3.table_ref, bf16[3,1536,128]{2,1,0:T(8,128)(2,1)} %qkv_ref.1, bf16[128,1536]{1,0:T(8,128)(2,1)} %out_weight_ref.1), custom_call_target="tpu_custom_call" | custom-call | tf_op jit(solution)/shard_map/pallas_call | solution.py:440
  68.7 1.8 %copy.13 = bf16[512,384]{1,0:T(8,128)(2,1)} copy(bf16[512,384]{1,0:T(8,128)(2,1)} %shard_map.64) | data formatting | bytes 786432
  (2 shorter events, 0.0 us)
Async XLA Ops:
  0.0 1.6 %copy-start = (f32[50,3,3072]{2,0,1:T(8,128)S(1)}, f32[50,3,3072]{2,0,1:T(8,128)}, u32[]{:S(2)}) copy-start(f32[50,3,3072]{2,0,1:T(8,128)} %param.9) | copy-start | bytes 5529604

commit v2 on v1

--- a/solution.py
+++ b/solution.py
@@ -94,10 +94,15 @@
 def fused_kernel(
     dims,
     tokens_ref,
-    table_ref,
+    step_ref,
+    padded_ref,
+    modulation_ref,
     qkv_ref,
     out_weight_ref,
     out_ref,
+    step_smem,
+    padded_smem,
+    modulation,
     tok,
     mod,
     wts,
@@ -105,6 +110,8 @@
     kv,
     att,
     wout,
+    outw,
+    table,
     local_sem,
     tok_send,
     tok_recv,
@@ -116,8 +123,6 @@
     att_recv,
     o_send,
     o_recv,
-    f_send,
-    f_recv,
 ):
     S, chunks, pieces = dims
     rows, width = tokens_ref.shape
@@ -239,33 +244,24 @@
     def o_at(head, p):
         return wout.at[head, pl.ds(pl.multiple_of(p * hpart, 16), hpart)]
 
-    def o_src(j):
-        return out_weight_ref.at[pl.ds(pl.multiple_of(g * hpart, 16), hpart), pl.ds(j * width, width)]
+    def o_over(block):
+        src = out_weight_ref.at[pl.ds(pl.multiple_of(g * hpart, 16), hpart)]
+        return remote(src, outw.at[block], o_send.at[0, 0], o_recv.at[0, 0], over)
 
     per_blk = slices // 2
-    home = own // per_blk == x
-
-    def o_copy(j):
-        s = x * per_blk + j
-        return remote(o_src(j), o_at(own, g), o_send.at[j], o_recv.at[own], (g, s // 2, x, s % 2))
-
-    def o_local(j):
-        return pltpu.make_async_copy(o_src(j), o_at(own, g), local_sem.at[5])
+
+    def o_src(s):
+        return outw.at[s // per_blk, :, lanes(lax.rem(s, per_blk), width)]
+
+    def o_copy(step):
+        s = lax.rem(own + step, slices)
+        return remote(o_src(s), o_at(own, g), o_send.at[1, step], o_recv.at[1, own], (g, s // 2, x, s % 2))
 
     def o_in(head):
-        return remote(o_at(head, g), o_at(head, g), o_send.at[0], o_recv.at[head], mate)
-
-    def o_all(p):
-        return wout.at[:, pl.ds(pl.multiple_of(p * hpart, 16), hpart)]
-
-    def f_over():
-        return remote(o_all(g), o_all(g), f_send.at[0], f_recv.at[0], over)
-
-    def f_twin():
-        return remote(o_all(g), o_all(g), f_send.at[1], f_recv.at[1], twin)
-
-    def f_twin_in():
-        return remote(o_all(1 - g), o_all(1 - g), f_send.at[1], f_recv.at[1], twin)
+        return remote(o_at(head, g), o_at(head, g), o_send.at[1, 0], o_recv.at[1, head], mate)
+
+    def o_twin(head, p):
+        return remote(o_at(head, p), o_at(head, p), o_send.at[2, head], o_recv.at[2, head], twin)
 
     def kv_at(block, r):
         return kv.at[block, :, pl.ds(r * R, R)]
@@ -279,7 +275,15 @@
         pl.semaphore_signal(barrier, inc=1, device_id=(g, s // 2, x, s % 2), device_id_type=MESH)
     for where in (over, twin):
         pl.semaphore_signal(barrier, inc=1, device_id=where, device_id_type=MESH)
-    locals_ = [pltpu.make_async_copy(tokens_ref, tok.at[:, lanes(own, width)], local_sem.at[0])]
+    locals_ = [
+        pltpu.make_async_copy(tokens_ref, tok.at[:, lanes(own, width)], local_sem.at[0]),
+        pltpu.make_async_copy(step_ref, step_smem, local_sem.at[6]),
+        pltpu.make_async_copy(padded_ref, padded_smem, local_sem.at[7]),
+        pltpu.make_async_copy(modulation_ref, modulation, local_sem.at[8]),
+        pltpu.make_async_copy(
+            out_weight_ref.at[pl.ds(pl.multiple_of(g * hpart, 16), hpart)], outw.at[x], local_sem.at[9]
+        ),
+    ]
     for i in range(kinds):
         there = wts.at[pl.ds(pl.multiple_of(x * half, 16), half), pl.ds(i * size, size)]
         locals_.append(pltpu.make_async_copy(qkv_ref.at[i], there, local_sem.at[1 + i]))
@@ -291,8 +295,13 @@
         send_own(tok_copy, r, tokens_ref.at[pl.ds(r * R, R)])
     for i in range(kinds):
         w_over(i).start()
+    o_over(x).start()
     for copy in locals_:
         copy.wait()
+    row = pl.ds(step_smem[0], 1)
+    table[0:1, :] = 1.0 + modulation[1, row, :]
+    table[1:2, :] = modulation[0, row, :]
+    table[2:3, :] = modulation[2, row, :]
 
     def normalise(r):
         group_rows = 16
@@ -304,7 +313,7 @@
             spread = jnp.mean(centered * centered, axis=1, keepdims=True)
             normed = centered * lax.rsqrt(spread + epsilon)
             to = pl.multiple_of(i * group_rows, group_rows)
-            mod[pl.ds(to, group_rows), :] = (normed * (1.0 + table_ref[1:2, :]) + table_ref[0:1, :]).astype(bf16)
+            mod[pl.ds(to, group_rows), :] = (normed * table[0:1, :] + table[1:2, :]).astype(bf16)
             return carry
 
         lax.fori_loop(0, R // group_rows, one, 0)
@@ -333,30 +342,22 @@
             if last and r > 0:
                 compute(r - 1)
         if d == S - 2:
-            for j in range(per_blk):
-                s = x * per_blk + j
-
-                @pl.when(s == own)
-                def _():
-                    o_local(j).start()
-
-                @pl.when(s != own)
-                def _():
-                    o_copy(j).start()
+            o_over(1 - x).wait_recv()
+            local = pltpu.make_async_copy(o_src(own), o_at(own, g), local_sem.at[5])
+            local.start()
+            for step in range(1, slices):
+                o_copy(step).start()
+            local.wait()
+            o_twin(own, g).start()
 
     compute(chunks - 1)
-    for j in range(per_blk):
-        s = x * per_blk + j
-
-        @pl.when(s == own)
-        def _():
-            o_local(j).wait()
-
     for r in range(chunks):
         kv_copy(1 - x, r).wait_recv()
 
     factor = 1.0 / math.sqrt(size)
     contract = (((1,), (1,)), ((), ()))
+
+    live = jnp.full((1, size), padded_smem[0], jnp.int32) < slices - own
 
     def attend(r):
         q = query[pl.ds(r * A, A), :]
@@ -372,37 +373,30 @@
             total = total + jnp.sum(weights, axis=1, keepdims=True)
             weighted = weighted + jnp.dot(weights.astype(bf16), kv[b, 1], preferred_element_type=f32)
         attended = weighted / total
-        masked = jnp.where(table_ref[3:4, :size] > 0.0, attended, 0.0).astype(bf16)
+        masked = jnp.where(live, attended, 0.0).astype(bf16)
         att[pl.ds(r * A, A), lanes(own, size)] = masked
         send_own(att_copy, r)
 
     for r in range(pieces):
         attend(r)
 
-    @pl.when(home)
-    def _():
-        for step in range(1, slices):
-            o_in(lax.rem(own + step, slices)).wait_recv()
-        f_over().start()
-        f_twin().start()
+    for step in range(1, slices):
+        head = lax.rem(own + step, slices)
+        o_in(head).wait_recv()
+        o_twin(head, g).start()
 
     for d in range(1, S):
         for r in range(pieces):
             relay(att_copy, d, r)
-        if d == 1:
-
-            @pl.when(jnp.logical_not(home))
-            def _():
-                f_over().wait_recv()
-                f_twin().start()
-
-    f_twin_in().wait_recv()
-    gate = table_ref[2:3, lanes(own, width)]
+
+    for head in range(slices):
+        o_twin(head, 1 - g).wait_recv()
+    gate = table[2:3, lanes(own, width)]
     weight = wout[...].reshape(slices * size, width)
     for r in range(pieces):
         wait_mates(att_copy, r)
         summed = jnp.dot(att[pl.ds(r * A, A), :], weight, preferred_element_type=f32)
-        out_ref[pl.ds(r * A, A), :] = (gate * summed).astype(bf16)
+        out_ref[pl.ds(r * A, A), :] = gate * summed
 
     drain(tok_copy, chunks)
     drain(att_copy, pieces)
@@ -411,18 +405,11 @@
         w_twin(i).wait_send()
     for r in range(chunks):
         kv_copy(x, r).wait_send()
-    for j in range(per_blk):
-        s = x * per_blk + j
-
-        @pl.when(s != own)
-        def _():
-            o_copy(j).wait_send()
-
-    f_twin().wait_send()
-
-    @pl.when(home)
-    def _():
-        f_over().wait_send()
+    o_over(x).wait_send()
+    for step in range(1, slices):
+        o_copy(step).wait_send()
+    for head in range(slices):
+        o_twin(head, g).wait_send()
 
 
 def fused_body(S, tokens, timestep, padded_heads, modulation, qkv_weight, out_weight):
@@ -431,18 +418,19 @@
     kinds, half, size = qkv_weight.shape
     model_width = modulation.shape[2]
     chunks, pieces = 4, 2
-    table_row = lax.dynamic_index_in_dim(modulation, timestep[0], 0, keepdims=False)
-    live = lax.axis_index(("seq", "tp")) < slices - padded_heads[0]
-    table = jnp.concatenate([table_row, jnp.full((1, model_width), live.astype(f32))], axis=0)
-    anywhere = pl.BlockSpec(memory_space=pl.ANY)
+    by_kind = jnp.transpose(modulation, (1, 0, 2))
+    anywhere = pl.BlockSpec(memory_space=pltpu.HBM)
     vmem = pl.BlockSpec(memory_space=pltpu.VMEM)
     dma = pltpu.SemaphoreType.DMA
-    return pl.pallas_call(
+    update = pl.pallas_call(
         functools.partial(fused_kernel, (S, chunks, pieces)),
-        out_shape=jax.ShapeDtypeStruct((rows, width), bf16),
-        in_specs=[anywhere, vmem, anywhere, anywhere],
+        out_shape=jax.ShapeDtypeStruct((rows, width), f32),
+        in_specs=[anywhere] * 6,
         out_specs=vmem,
         scratch_shapes=[
+            pltpu.SMEM((1,), jnp.int32),
+            pltpu.SMEM((1,), jnp.int32),
+            pltpu.VMEM(by_kind.shape, f32),
             pltpu.VMEM((rows, model_width), bf16),
             pltpu.VMEM((rows // chunks, model_width), bf16),
             pltpu.VMEM((model_width, kinds * size), bf16),
@@ -450,7 +438,9 @@
             pltpu.VMEM((2, 2, rows, size), bf16),
             pltpu.VMEM((rows, slices * size), bf16),
             pltpu.VMEM((slices, size, width), bf16),
-            dma((6,)),
+            pltpu.VMEM((2, size // 2, out_weight.shape[1]), bf16),
+            pltpu.VMEM((8, model_width), f32),
+            dma((10,)),
             dma((3, slices, chunks)),
             dma((slices, chunks)),
             dma((2, kinds)),
@@ -459,13 +449,12 @@
             dma((chunks,)),
             dma((3, slices, pieces)),
             dma((slices, pieces)),
-            dma((slices // 2,)),
-            dma((slices,)),
-            dma((2,)),
-            dma((2,)),
+            dma((3, slices)),
+            dma((3, slices)),
         ],
         compiler_params=pltpu.CompilerParams(collective_id=0, has_side_effects=True),
-    )(tokens, table, qkv_weight, out_weight)
+    )(tokens, timestep, padded_heads, by_kind, qkv_weight, out_weight)
+    return update.astype(bf16)
 
 
 def fits(mesh):

time: 70.7 us -> 65.1 us (0.921)
  the two profiles are of different devices: /device:TPU:2 before, /device:TPU:0 now
where the time goes in v2:
time: 65.1 us; the launch traced here: 64.7 us
  Pallas kernels  61.5 us (94%)
  other arithmetic  1.92 us (3%)
  between operations  1.3 us (2%)
    pallas_call x1, Pallas kernels, fused_body(): pl.pallas_call(functools.partial(fused_kernel, (S, chunks, pieces)), out_...  61.5 us
    convert_element_type x1, other arithmetic, fused_body(): return update.astype(bf16)  1.92 us

profile of v2, /device:TPU:0, one launch (start us, length us, event | category | flops | bytes accessed | tf_op | source)
XLA Modules:
  0.0 64.7 jit_solution(7487988077729689705)
XLA Ops:
  1.3 61.5 %shard_map.64 = f32[512,384]{1,0:T(8,128)} custom-call(bf16[512,384]{1,0:T(8,128)(2,1)} %tokens_ref.1, s32[1]{0:T(128)S(6)} %copy.7.step_ref, s32[1]{0:T(128)S(6)} %copy.8.padded_ref, f32[3,50,3072]{2,1,0:T(8,128)} %bitcast.1, bf16[3,1536,128]{2,1,0:T(8,128)(2,1)} %qkv_ref.1, bf16[128,1536]{1,0:T(8,128)(2,1)} %out_weight_ref.1), custom_call_target="tpu_custom_call" | custom-call | tf_op jit(solution)/shard_map/pallas_call | solution.py:425
  62.8 1.9 %convert_element_type.3 = bf16[512,384]{1,0:T(8,128)(2,1)} convert(f32[512,384]{1,0:T(8,128)} %shard_map.64) | non-fusion elementwise | flops 196608 | bytes 1179648 | tf_op jit(solution)/shard_map/convert_element_type | solution.py:457

commit v3 on v2

--- a/solution.py
+++ b/solution.py
@@ -112,6 +112,12 @@
     wout,
     outw,
     table,
+    lift,
+    vectors,
+    level,
+    sums,
+    squares,
+    total,
     local_sem,
     tok_send,
     tok_recv,
@@ -303,31 +309,79 @@
     table[1:2, :] = modulation[0, row, :]
     table[2:3, :] = modulation[2, row, :]
 
-    def normalise(r):
-        group_rows = 16
+    block = 32
+    span = 2 * width
+    tile = level.shape[1]
+
+    def fold(values):
+        folded = values[:, :tile]
+        for i in range(1, values.shape[1] // tile):
+            folded = folded + values[:, i * tile : (i + 1) * tile]
+        return folded
+
+    def set_level(i, carry):
+        at = pl.ds(pl.multiple_of(i * block, block), block)
+        values = tok[at, lanes(own, width)].astype(f32)
+        level[at, :] = jnp.broadcast_to(jnp.mean(values, axis=1, keepdims=True), (block, tile))
+        return carry
+
+    lax.fori_loop(0, rows // block, set_level, 0)
+    lift[...] = jnp.zeros_like(lift)
+    for i in range(2):
+        high = table[i : i + 1, :].astype(bf16).astype(f32)
+        lift[2 * i : 2 * i + 1, :] = high
+        lift[2 * i + 1 : 2 * i + 2, :] = table[i : i + 1, :] - high
+
+    def set_vectors():
+        for i in range(kinds):
+            w_twin_in(i).wait_recv()
+        product = jnp.dot(lift[...].astype(bf16), wts[...], preferred_element_type=f32)
+        vectors[0:1, :] = product[0:1] + product[1:2]
+        vectors[1:2, :] = product[2:3] + product[3:4]
+
+    def add_pair(chip, r, count, first=False):
+        for i in range(r, r + count):
+            tok_copy(2, chip * 2 + 1 - c, i, mate).wait_recv()
+        columns = lanes(chip, span)
 
         def one(i, carry):
-            at = pl.multiple_of(r * R + i * group_rows, group_rows)
-            values = tok[pl.ds(at, group_rows), :].astype(f32)
-            centered = values - jnp.mean(values, axis=1, keepdims=True)
-            spread = jnp.mean(centered * centered, axis=1, keepdims=True)
-            normed = centered * lax.rsqrt(spread + epsilon)
-            to = pl.multiple_of(i * group_rows, group_rows)
-            mod[pl.ds(to, group_rows), :] = (normed * table[0:1, :] + table[1:2, :]).astype(bf16)
+            at = pl.ds(pl.multiple_of(r * R + i * block, block), block)
+            base = level[at, :]
+            shifted = tok[at, columns].astype(f32) - jnp.concatenate([base] * (span // tile), axis=1)
+            if first:
+                sums[at, :] = fold(shifted)
+                squares[at, :] = fold(shifted * shifted)
+            else:
+                sums[at, :] += fold(shifted)
+                squares[at, :] += fold(shifted * shifted)
+            mod[pl.ds(pl.multiple_of(i * block, block), block), :] = (shifted * table[0:1, columns]).astype(bf16)
             return carry
 
-        lax.fori_loop(0, R // group_rows, one, 0)
-
-    def compute(r):
-        wait_mates(tok_copy, r)
-        normalise(r)
-        if r == 0:
-            for i in range(kinds):
-                w_twin_in(i).wait_recv()
-        projected = jnp.dot(mod[...], wts[...], preferred_element_type=f32).astype(bf16)
-        query[pl.ds(r * R, R), :] = projected[:, :size]
-        kv[x, 0, pl.ds(r * R, R), :] = projected[:, size : 2 * size]
-        kv[x, 1, pl.ds(r * R, R), :] = projected[:, 2 * size :]
+        lax.fori_loop(0, count * R // block, one, 0)
+        depth = pl.ds(pl.multiple_of(chip * span, 16), span)
+        at = pl.ds(r * R, count * R)
+        product = jnp.dot(mod[: count * R, :], wts[depth, :], preferred_element_type=f32)
+        total[at, :] = product if first else total[at, :] + product
+
+    def add_ring(d, r, count):
+        @pl.when(z - d >= 0)
+        def _():
+            add_pair(z - d, r, count)
+
+        @pl.when(z + d < S)
+        def _():
+            add_pair(z + d, r, count)
+
+    def finish(r):
+        at = pl.ds(r * R, R)
+        share = 1.0 / (slices * width)
+        offset = jnp.sum(sums[at, :], axis=1, keepdims=True) * share
+        spread = jnp.sum(squares[at, :], axis=1, keepdims=True) * share - offset * offset
+        rate = lax.rsqrt(jnp.maximum(spread, 0.0) + epsilon)
+        projected = ((total[at, :] - offset * vectors[0:1, :]) * rate + vectors[1:2, :]).astype(bf16)
+        query[at, :] = projected[:, :size]
+        kv[x, 0, at, :] = projected[:, size : 2 * size]
+        kv[x, 1, at, :] = projected[:, 2 * size :]
         kv_copy(x, r).start()
 
     forwarded = 0
@@ -339,18 +393,29 @@
                 w_over_in(forwarded).wait_recv()
                 w_twin(forwarded).start()
                 forwarded += 1
-            if last and r > 0:
-                compute(r - 1)
+            if last:
+                add_ring(d - 1, r, 1)
+                if r > 0:
+                    add_ring(d, r - 1, 1)
+                    finish(r - 1)
         if d == S - 2:
-            o_over(1 - x).wait_recv()
-            local = pltpu.make_async_copy(o_src(own), o_at(own, g), local_sem.at[5])
-            local.start()
-            for step in range(1, slices):
-                o_copy(step).start()
-            local.wait()
-            o_twin(own, g).start()
-
-    compute(chunks - 1)
+            set_vectors()
+            for r in range(0, chunks, 2):
+                add_pair(z, r, 2, True)
+            for near in range(1, d):
+                for r in range(0, chunks, 2):
+                    add_ring(near, r, 2)
+
+    o_over(1 - x).wait_recv()
+    local = pltpu.make_async_copy(o_src(own), o_at(own, g), local_sem.at[5])
+    local.start()
+    for step in range(1, slices):
+        o_copy(step).start()
+    add_ring(S - 1, chunks - 1, 1)
+    finish(chunks - 1)
+    local.wait()
+    o_twin(own, g).start()
+
     for r in range(chunks):
         kv_copy(1 - x, r).wait_recv()
 
@@ -380,14 +445,14 @@
     for r in range(pieces):
         attend(r)
 
-    for step in range(1, slices):
-        head = lax.rem(own + step, slices)
-        o_in(head).wait_recv()
-        o_twin(head, g).start()
-
     for d in range(1, S):
         for r in range(pieces):
             relay(att_copy, d, r)
+        if d == 1:
+            for step in range(1, slices):
+                head = lax.rem(own + step, slices)
+                o_in(head).wait_recv()
+                o_twin(head, g).start()
 
     for head in range(slices):
         o_twin(head, 1 - g).wait_recv()
@@ -432,7 +497,7 @@
             pltpu.SMEM((1,), jnp.int32),
             pltpu.VMEM(by_kind.shape, f32),
             pltpu.VMEM((rows, model_width), bf16),
-            pltpu.VMEM((rows // chunks, model_width), bf16),
+            pltpu.VMEM((2 * rows // chunks, 2 * width), bf16),
             pltpu.VMEM((model_width, kinds * size), bf16),
             pltpu.VMEM((rows, size), bf16),
             pltpu.VMEM((2, 2, rows, size), bf16),
@@ -440,6 +505,12 @@
             pltpu.VMEM((slices, size, width), bf16),
             pltpu.VMEM((2, size // 2, out_weight.shape[1]), bf16),
             pltpu.VMEM((8, model_width), f32),
+            pltpu.VMEM((8, model_width), f32),
+            pltpu.VMEM((8, kinds * size), f32),
+            pltpu.VMEM((rows, 128), f32),
+            pltpu.VMEM((rows, 128), f32),
+            pltpu.VMEM((rows, 128), f32),
+            pltpu.VMEM((rows, kinds * size), f32),
             dma((10,)),
             dma((3, slices, chunks)),
             dma((slices, chunks)),
@@ -459,7 +530,7 @@
 
 def fits(mesh):
     shape = mesh.shape
-    return shape["group"] == 2 and shape["blk"] == 2 and shape["tp"] == 2 and shape["seq"] >= 3
+    return shape["group"] == 2 and shape["blk"] == 2 and shape["tp"] == 2 and shape["seq"] >= 4
 
 
 def solution(mesh):

time: 65.1 us -> 59.4 us (0.912)
  Pallas kernels: 61.5 us -> 55.7 us
    pallas_call x1, Pallas kernels: 61.5 us -> 55.7 us  [fused_body(): pl.pallas_call(functools.partial(fused_kernel, (S, chunks, pieces)), out_...]
where the time goes in v3:
time: 59.4 us; the launch traced here: 59 us
  Pallas kernels  55.7 us (94%)
  other arithmetic  1.92 us (3%)
  between operations  1.3 us (2%)
    pallas_call x1, Pallas kernels, fused_body(): pl.pallas_call(functools.partial(fused_kernel, (S, chunks, pieces)), out_...  55.7 us
    convert_element_type x1, other arithmetic, fused_body(): return update.astype(bf16)  1.92 us

profile of v3, /device:TPU:0, one launch (start us, length us, event | category | flops | bytes accessed | tf_op | source)
XLA Modules:
  0.0 59.0 jit_solution(17654087620865375392)
XLA Ops:
  1.3 55.7 %shard_map.64 = f32[512,384]{1,0:T(8,128)} custom-call(bf16[512,384]{1,0:T(8,128)(2,1)} %tokens_ref.1, s32[1]{0:T(128)S(6)} %copy.7.step_ref, s32[1]{0:T(128)S(6)} %copy.8.padded_ref, f32[3,50,3072]{2,1,0:T(8,128)} %bitcast.1, bf16[3,1536,128]{2,1,0:T(8,128)(2,1)} %qkv_ref.1, bf16[128,1536]{1,0:T(8,128)(2,1)} %out_weight_ref.1), custom_call_target="tpu_custom_call" | custom-call | tf_op jit(solution)/shard_map/pallas_call | solution.py:490
  57.1 1.9 %convert_element_type.3 = bf16[512,384]{1,0:T(8,128)(2,1)} convert(f32[512,384]{1,0:T(8,128)} %shard_map.64) | non-fusion elementwise | flops 196608 | bytes 1179648 | tf_op jit(solution)/shard_map/convert_element_type | solution.py:528

commit v4 on v3

--- a/solution.py
+++ b/solution.py
@@ -384,6 +384,14 @@
         kv[x, 1, at, :] = projected[:, 2 * size :]
         kv_copy(x, r).start()
 
+    def send_out_weight(inner):
+        for step in range(1, slices):
+            chip = lax.rem(own + step, slices) // 2
+
+            @pl.when(((chip > 0) & (chip < S - 1)) == inner)
+            def _():
+                o_copy(step).start()
+
     forwarded = 0
     for d in range(1, S):
         last = d == S - 1
@@ -400,25 +408,22 @@
                     finish(r - 1)
         if d == S - 2:
             set_vectors()
+            o_over(1 - x).wait_recv()
+            local = pltpu.make_async_copy(o_src(own), o_at(own, g), local_sem.at[5])
+            local.start()
+            send_out_weight(True)
             for r in range(0, chunks, 2):
                 add_pair(z, r, 2, True)
             for near in range(1, d):
                 for r in range(0, chunks, 2):
                     add_ring(near, r, 2)
 
-    o_over(1 - x).wait_recv()
-    local = pltpu.make_async_copy(o_src(own), o_at(own, g), local_sem.at[5])
-    local.start()
-    for step in range(1, slices):
-        o_copy(step).start()
+    send_out_weight(False)
     add_ring(S - 1, chunks - 1, 1)
     finish(chunks - 1)
     local.wait()
     o_twin(own, g).start()
 
-    for r in range(chunks):
-        kv_copy(1 - x, r).wait_recv()
-
     factor = 1.0 / math.sqrt(size)
     contract = (((1,), (1,)), ((), ()))
 
@@ -426,15 +431,18 @@
 
     def attend(r):
         q = query[pl.ds(r * A, A), :]
-        scores = [
-            lax.dot_general(q, kv[b, 0], contract, preferred_element_type=f32) * factor for b in range(2)
-        ]
+        scores = []
+        for b in (x, 1 - x):
+            if r == 0 and len(scores) > 0:
+                for i in range(chunks):
+                    kv_copy(1 - x, i).wait_recv()
+            scores.append(lax.dot_general(q, kv[b, 0], contract, preferred_element_type=f32) * factor)
         largest = jnp.maximum(
             jnp.max(scores[0], axis=1, keepdims=True), jnp.max(scores[1], axis=1, keepdims=True)
         )
         total, weighted = 0.0, 0.0
-        for b in range(2):
-            weights = jnp.exp(scores[b] - largest)
+        for b, part_scores in zip((x, 1 - x), scores):
+            weights = jnp.exp(part_scores - largest)
             total = total + jnp.sum(weights, axis=1, keepdims=True)
             weighted = weighted + jnp.dot(weights.astype(bf16), kv[b, 1], preferred_element_type=f32)
         attended = weighted / total
@@ -461,7 +469,7 @@
     for r in range(pieces):
         wait_mates(att_copy, r)
         summed = jnp.dot(att[pl.ds(r * A, A), :], weight, preferred_element_type=f32)
-        out_ref[pl.ds(r * A, A), :] = gate * summed
+        out_ref[pl.ds(r * A, A), :] = (gate * summed).astype(bf16)
 
     drain(tok_copy, chunks)
     drain(att_copy, pieces)
@@ -482,14 +490,14 @@
     rows, width = tokens.shape
     kinds, half, size = qkv_weight.shape
     model_width = modulation.shape[2]
-    chunks, pieces = 4, 2
+    chunks, pieces = 4, 4
     by_kind = jnp.transpose(modulation, (1, 0, 2))
     anywhere = pl.BlockSpec(memory_space=pltpu.HBM)
     vmem = pl.BlockSpec(memory_space=pltpu.VMEM)
     dma = pltpu.SemaphoreType.DMA
-    update = pl.pallas_call(
+    return pl.pallas_call(
         functools.partial(fused_kernel, (S, chunks, pieces)),
-        out_shape=jax.ShapeDtypeStruct((rows, width), f32),
+        out_shape=jax.ShapeDtypeStruct((rows, width), bf16),
         in_specs=[anywhere] * 6,
         out_specs=vmem,
         scratch_shapes=[
@@ -525,7 +533,6 @@
         ],
         compiler_params=pltpu.CompilerParams(collective_id=0, has_side_effects=True),
     )(tokens, timestep, padded_heads, by_kind, qkv_weight, out_weight)
-    return update.astype(bf16)
 
 
 def fits(mesh):

time: 59.4 us -> 60.3 us (1.015)
  other arithmetic: 1.92 us -> 0 us
  local copies, waits for them, and re-layouts: 0 us -> 1.78 us
  Pallas kernels: 55.7 us -> 56.4 us
    convert_element_type x1 -> x0, other arithmetic: 1.92 us -> none  [fused_body(): return update.astype(bf16)]
    unnamed x0 -> x1, local copies, waits for them, and re-layouts: none -> 1.78 us
    pallas_call x1, Pallas kernels: 55.7 us -> 56.4 us  [fused_body(): pl.pallas_call(functools.partial(fused_kernel, (S, chunks, pieces)), out_...]
where the time goes in v4:
time: 60.3 us; the launch traced here: 59.5 us
  Pallas kernels  56.4 us (94%)
  local copies, waits for them, and re-layouts  1.78 us (3%)
  between operations  1.3 us (2%)
    pallas_call x1, Pallas kernels, fused_body(): pl.pallas_call(functools.partial(fused_kernel, (S, chunks, pieces)), out_...  56.4 us
    unnamed x1, local copies, waits for them, and re-layouts  1.78 us

profile of v4, /device:TPU:0, one launch (start us, length us, event | category | flops | bytes accessed | tf_op | source)
XLA Modules:
  0.0 59.5 jit_solution(15540571806216733589)
XLA Ops:
  1.3 56.4 %shard_map.64 = bf16[512,384]{1,0:T(8,128)(2,1)} custom-call(bf16[512,384]{1,0:T(8,128)(2,1)} %tokens_ref.1, s32[1]{0:T(128)S(6)} %copy.8.step_ref, s32[1]{0:T(128)S(6)} %copy.9.padded_ref, f32[3,50,3072]{2,1,0:T(8,128)} %bitcast.1, bf16[3,1536,128]{2,1,0:T(8,128)(2,1)} %qkv_ref.1, bf16[128,1536]{1,0:T(8,128)(2,1)} %out_weight_ref.1), custom_call_target="tpu_custom_call" | custom-call | tf_op jit(solution)/shard_map/pallas_call | solution.py:498
  57.7 1.8 %copy.10 = bf16[512,384]{1,0:T(8,128)(2,1)} copy(bf16[512,384]{1,0:T(8,128)(2,1)} %shard_map.64) | data formatting | bytes 786432

commit v5 on v4

--- a/solution.py
+++ b/solution.py
@@ -276,10 +276,16 @@
         return remote(kv_at(block, r), kv_at(block, r), kv_send.at[r], kv_recv.at[r], over)
 
     barrier = pltpu.get_barrier_semaphore()
-    for step in range(1, slices):
-        s = lax.rem(own + step, slices)
-        pl.semaphore_signal(barrier, inc=1, device_id=(g, s // 2, x, s % 2), device_id_type=MESH)
-    for where in (over, twin):
+
+    @pl.when(z < S - 1)
+    def _():
+        pl.semaphore_signal(barrier, inc=1, device_id=up, device_id_type=MESH)
+
+    @pl.when(z > 0)
+    def _():
+        pl.semaphore_signal(barrier, inc=1, device_id=down, device_id_type=MESH)
+
+    for where in (mate, over, twin):
         pl.semaphore_signal(barrier, inc=1, device_id=where, device_id_type=MESH)
     locals_ = [
         pltpu.make_async_copy(tokens_ref, tok.at[:, lanes(own, width)], local_sem.at[0]),
@@ -295,7 +301,7 @@
         locals_.append(pltpu.make_async_copy(qkv_ref.at[i], there, local_sem.at[1 + i]))
     for copy in locals_:
         copy.start()
-    pl.semaphore_wait(barrier, slices + 1)
+    pl.semaphore_wait(barrier, 3 + (z < S - 1).astype(jnp.int32) + (z > 0).astype(jnp.int32))
 
     for r in range(chunks):
         send_own(tok_copy, r, tokens_ref.at[pl.ds(r * R, R)])
@@ -490,7 +496,7 @@
     rows, width = tokens.shape
     kinds, half, size = qkv_weight.shape
     model_width = modulation.shape[2]
-    chunks, pieces = 4, 4
+    chunks, pieces = 4, 2
     by_kind = jnp.transpose(modulation, (1, 0, 2))
     anywhere = pl.BlockSpec(memory_space=pltpu.HBM)
     vmem = pl.BlockSpec(memory_space=pltpu.VMEM)

time: 60.3 us -> 57.8 us (0.959)
  Pallas kernels: 56.4 us -> 54.3 us
    pallas_call x1, Pallas kernels: 56.4 us -> 54.3 us  [fused_body(): pl.pallas_call(functools.partial(fused_kernel, (S, chunks, pieces)), out_...]
where the time goes in v5:
time: 57.8 us; the launch traced here: 57.4 us
  Pallas kernels  54.3 us (94%)
  local copies, waits for them, and re-layouts  1.78 us (3%)
  between operations  1.3 us (2%)
    pallas_call x1, Pallas kernels, fused_body(): pl.pallas_call(functools.partial(fused_kernel, (S, chunks, pieces)), out_...  54.3 us
    unnamed x1, local copies, waits for them, and re-layouts  1.78 us

profile of v5, /device:TPU:0, one launch (start us, length us, event | category | flops | bytes accessed | tf_op | source)
XLA Modules:
  0.0 57.4 jit_solution(8956364040383759286)
XLA Ops:
  1.3 54.3 %shard_map.64 = bf16[512,384]{1,0:T(8,128)(2,1)} custom-call(bf16[512,384]{1,0:T(8,128)(2,1)} %tokens_ref.1, s32[1]{0:T(128)S(6)} %copy.8.step_ref, s32[1]{0:T(128)S(6)} %copy.9.padded_ref, f32[3,50,3072]{2,1,0:T(8,128)} %bitcast.1, bf16[3,1536,128]{2,1,0:T(8,128)(2,1)} %qkv_ref.1, bf16[128,1536]{1,0:T(8,128)(2,1)} %out_weight_ref.1), custom_call_target="tpu_custom_call" | custom-call | tf_op jit(solution)/shard_map/pallas_call | solution.py:504
  55.6 1.8 %copy.10 = bf16[512,384]{1,0:T(8,128)(2,1)} copy(bf16[512,384]{1,0:T(8,128)(2,1)} %shard_map.64) | data formatting | bytes 786432
